TPU v7x, 32 devices: a whole 2x2x4 slice. The times are simulated.
32 devices in a mesh: groups: 2 (over y), gx: 4 (over z), gy: 2 (over x), gz: 2 (over core).
Axes of the slice: x: 2, y: 2, z: 4, core: 2. Of those that a mesh axis runs over, the one named last changes fastest.
Arguments:
- features: bfloat16 [32, 8, 32, 128], P(('groups', 'gx'), 'gy', 'gz'), parts along dimension 0, may hold values from -6 to 6
- scales: bfloat16 [32, 8, 32, 128], P(('groups', 'gx'), 'gy', 'gz'), parts along dimension 0, may hold values from 0.29882812 to 3
- occupancy: int32 [8, 2, 8], P(('groups', 'gx'), 'gy', 'gz'), parts along dimension 0, may hold values 0 or 1
- kernel: bfloat16 [62, 128, 128], replicated, may hold values from -0.0625 to 0.0625
- gamma: float32 [128, 128], replicated, may hold values from 0 to 0.015625
- beta: float32 [128], replicated, may hold values from 0.5 to 2
Outputs:
- grad_features: bfloat16 [32, 8, 32, 128], P(('groups', 'gx'), 'gy', 'gz'), parts along dimension 0
- grad_kernel: float32 [2031616], P(('groups', 'gx', 'gy', 'gz')), parts along dimension 0
- grad_gamma: float32 [256, 128], P('groups'), parts along dimension 0
- grad_beta: float32 [256], P('groups'), parts along dimension 0
There are 2 independent parts, one for each index of `groups`. A program takes and returns all parts, laid end to end along the dimension named above; an argument that names none is the same for every part. Nothing has to cross between parts.
All inputs are finite; a program needn't handle non-finite values. No bound on the sum of `occupancy` on one device may be relied on, other than what follows from the above.
Results may differ from a plain program's by a relative error of at most 0.0039.
The roundings to bfloat16 on the way count: a program that leaves them out, or rounds other values in their place, can miss the bound.
Values may be sent and summed in bfloat16 or wider, within the bound.
No kernel may reach another device: no remote copies, remote signals or barrier semaphores. Data moves between devices by JAX's collectives and lax.ppermute only.
A program may use at most 64 MiB of HBM per device.

v0:
```python
import math
import jax
import jax.numpy as jnp
from jax import lax
from jax.sharding import PartitionSpec as P

OB = 4


def padded_2(shard, sides, width):
    for axis, dim in sides:
        size, length = (lax.axis_size(axis), shard.shape[dim])
        up = [(i, (i + 1) % size) for i in range(size - 1)]
        down = [(j, i) for i, j in up]
        last = lax.slice_in_dim(shard, length - width, length, axis=dim)
        leading = lax.slice_in_dim(shard, 0, width, axis=dim)
        before = lax.ppermute(last, axis, up)
        after = lax.ppermute(leading, axis, down)
        shard = jnp.concatenate([before, shard, after], axis=dim)
    return shard


def from_behind(value, axis, steps):
    count = lax.axis_size(axis)
    leading, last = (max(0, -steps), min(count, count - steps))
    return lax.ppermute(value, axis, [(source, source + steps) for source in range(leading, last)])


def causal_offsets():
    result = []
    for along_x in range(-2, 3):
        for along_y in range(-2, 3):
            for along_z in range(-2, 3):
                if (along_x, along_y, along_z) < (0, 0, 0):
                    result.append((along_x, along_y, along_z))
    return result


def tap_groups():
    groups = []
    for number, offset in enumerate(causal_offsets()):
        if groups and groups[-1][0] == offset[0] and (groups[-1][1] == offset[1]):
            groups[-1][3] += 1
        else:
            groups.append([offset[0], offset[1], offset[2], 1, number])
    return groups


def expand_blocks(occupancy, edge):
    blocks_x, blocks_y, blocks_z = occupancy.shape
    grown = jnp.broadcast_to(
        occupancy[:, None, :, None, :, None], (blocks_x, edge, blocks_y, edge, blocks_z, edge)
    )
    return grown.reshape(-1, 1).astype(jnp.float32)


def forward_patch(padded, along_x, along_y, start_z, count, extent):
    size_x, size_y, size_z = extent
    pieces = [
        padded[
            2 + along_x : 2 + along_x + size_x,
            2 + along_y : 2 + along_y + size_y,
            2 + along_z : 2 + along_z + size_z,
        ]
        for along_z in range(start_z, start_z + count)
    ]
    return jnp.concatenate(pieces, axis=3).reshape(size_x * size_y * size_z, -1)


def context_mean(padded, kernel, extent):
    channels = kernel.shape[1]
    total = jnp.zeros((extent[0] * extent[1] * extent[2], channels), jnp.float32)
    for along_x, along_y, start_z, count, first_tap in tap_groups():
        patch = forward_patch(padded, along_x, along_y, start_z, count, extent)
        weights = kernel[first_tap : first_tap + count].reshape(count * channels, channels)
        total = total + jnp.dot(patch, weights, preferred_element_type=jnp.float32)
    return total


def context_transposed(padded, kernel, extent):
    size_x, size_y, size_z = extent
    channels = kernel.shape[1]
    total = jnp.zeros((size_x * size_y * size_z, channels), jnp.float32)
    for along_x, along_y, start_z, count, first_tap in tap_groups():
        pieces = [
            padded[
                -along_x : -along_x + size_x,
                2 - along_y : 2 - along_y + size_y,
                2 - along_z : 2 - along_z + size_z,
            ]
            for along_z in range(start_z, start_z + count)
        ]
        patch = jnp.concatenate(pieces, axis=3).reshape(size_x * size_y * size_z, -1)
        weights = jnp.transpose(kernel[first_tap : first_tap + count], (0, 2, 1)).reshape(
            count * channels, channels
        )
        total = total + jnp.dot(patch, weights, preferred_element_type=jnp.float32)
    return total


def kernel_terms(padded, mean_grad, extent):
    terms = []
    for along_x, along_y, start_z, count, first_tap in tap_groups():
        patch = forward_patch(padded, along_x, along_y, start_z, count, extent)
        terms.append(
            lax.dot_general(
                patch, mean_grad, (((0,), (0,)), ((), ())), preferred_element_type=jnp.float32
            )
        )
    return jnp.concatenate(terms, axis=0).reshape(-1)


def lower_sides_first(latent):
    widened = padded_2(latent, (("gy", 1), ("gz", 2)), 2)
    below = from_behind(widened[-2:], "gx", 1)
    return jnp.concatenate([below, widened], axis=0)


def upper_sides_first(grads):
    widened = padded_2(grads, (("gy", 1), ("gz", 2)), 2)
    above = from_behind(widened[:2], "gx", -1)
    return jnp.concatenate([widened, above], axis=0)


def local(features, scales, occupancy, kernel, gamma, beta):
    size_x, size_y, size_z, channels = features.shape
    extent = (size_x, size_y, size_z)
    voxels = size_x * size_y * size_z
    feats = features.astype(jnp.float32).reshape(voxels, channels)
    occupied = expand_blocks(occupancy, OB)
    energy = beta[None, :] + jnp.dot(
        feats * feats, gamma, precision=lax.Precision.HIGHEST, preferred_element_type=jnp.float32
    )
    inv_root = lax.rsqrt(energy)
    latent = (occupied * feats * inv_root).astype(jnp.bfloat16)
    latent_grid = latent.reshape(size_x, size_y, size_z, channels)
    padded = lower_sides_first(latent_grid)
    mean = context_mean(padded, kernel, extent)
    latent_f = latent.astype(jnp.float32)
    scale_f = scales.astype(jnp.float32).reshape(voxels, channels)
    inverse = 1.0 / (scale_f * scale_f)
    mean_grad = (occupied * (mean - latent_f) * inverse).astype(jnp.bfloat16)
    grad_grid = mean_grad.reshape(size_x, size_y, size_z, channels)
    grad_pad = upper_sides_first(grad_grid)
    context_grad = context_transposed(grad_pad, kernel, extent)
    latent_grad = occupied * (context_grad + (latent_f - mean) * inverse)
    weighted = latent_grad * feats * inv_root * inv_root * inv_root
    coupled = jnp.dot(
        weighted, gamma.T, precision=lax.Precision.HIGHEST, preferred_element_type=jnp.float32
    )
    grad_features = (
        (latent_grad * inv_root - feats * coupled)
        .astype(jnp.bfloat16)
        .reshape(size_x, size_y, size_z, channels)
    )
    kernel_local = kernel_terms(padded, mean_grad, extent) / voxels
    grad_kernel = lax.psum_scatter(
        kernel_local, ("gx", "gy", "gz"), scatter_dimension=0, tiled=True
    )
    factor = 0.5 / math.sqrt(voxels)
    gamma_local = -factor * jnp.dot(
        (feats * feats).T,
        weighted,
        precision=lax.Precision.HIGHEST,
        preferred_element_type=jnp.float32,
    )
    beta_local = -factor * jnp.sum(weighted, axis=0)
    grad_gamma, grad_beta = lax.psum((gamma_local, beta_local), ("gx", "gy", "gz"))
    return (grad_features, grad_kernel, grad_gamma, grad_beta)


def solution(mesh):
    return jax.shard_map(
        local,
        mesh=mesh,
        in_specs=(
            P(("groups", "gx"), "gy", "gz", None),
            P(("groups", "gx"), "gy", "gz", None),
            P(("groups", "gx"), "gy", "gz"),
            P(),
            P(),
            P(),
        ),
        out_specs=(
            P(("groups", "gx"), "gy", "gz", None),
            P(("groups", "gx", "gy", "gz")),
            P("groups", None),
            P("groups"),
        ),
        check_vma=False,
    )
```

profile of v0, /device:TPU:0, one launch (start us, length us, event | category | flops | bytes accessed | tf_op | source)
XLA Modules:
  0.0 195.3 jit_solution(11821745433101948663)
XLA Ops:
  7.2 0.7 convert_bitcast_fusion
  8.1 1.2 fusion.12
  9.3 4.9 %collective-permute-start = (bf16[4,2,16,128]{3,2,1,0:T(8,128)(2,1)S(1)}, bf16[4,2,16,128]{3,2,1,0:T(8,128)(2,1)S(1)}, u32[]{:S(2)}, u32[]{:S(2)}) collective-permute-start(bf16[4,2,16,128]{3,2,1,0:T(8,128)(2,1)S(1)} %get-tuple-element.160), channel_id=1, source_target_pairs={{0,2},{1,3},{4,6},{5,7},{8,10},{9,11},{12,14},{13,15},{16,18},{17,... | collective-permute-start | bytes 98312 | tf_op jit(solution)/shard_map/ppermute | solution.py:17
  14.2 1.3 collective-permute-start.1
  15.5 2.1 %fusion.16 = (bf16[5,128,128]{2,1,0:T(8,128)(2,1)}, bf16[5,128,128]{2,1,0:T(8,128)(2,1)}, bf16[5,128,128]{2,1,0:T(8,128)(2,1)}, bf16[5,128,128]{2,1,0:T(8,128)(2,1)}, bf16[5,128,128]{2,1,0:T(8,128)(2,1)}) fusion(bf16[62,128,128]{2,1,0:T(8,128)(2,1)} %param.9), kind=kLoop, calls=%fused_computation.225 | loop fusion | bytes 1638400 | tf_op jit(solution)/shard_map/slice | solution.py:75
  17.7 3.0 %slice_bitcast_fusion.1 = (bf16[5,128,128]{1,2,0:T(8,128)(2,1)S(1)}, bf16[5,128,128]{1,2,0:T(8,128)(2,1)S(1)}, bf16[5,128,128]{1,2,0:T(8,128)(2,1)S(1)}, bf16[5,...) fusion(bf16[62,128,128]{2,1,0:T(8,128)(2,1)} %param.9), kind=kLoop, calls=%fused_computation.212 | loop fusion | bytes 5079040 | tf_op jit(solution)/shard_map/transpose | solution.py:94
  20.6 0.9 slice_bitcast_fusion
  21.5 0.6 pad_maximum_fusion.18
  22.2 1.3 collective-permute-start.3
  23.5 3.6 %collective-permute-start.2 = (bf16[4,8,2,128]{3,2,1,0:T(2,128)(2,1)}, bf16[4,8,2,128]{3,2,1,0:T(2,128)(2,1)}, u32[]{:S(2)}, u32[]{:S(2)}) collective-permute-start(bf16[4,8,2,128]{3,2,1,0:T(2,128)(2,1)} %get-tuple-element.153), channel_id=1, source_target_pairs={{0,1},{2,3},{4,5},{6,7},{8,9},{10,11},{12,13},{14,15},{16,17},{18,... | collective-permute-start | bytes 49160 | tf_op jit(solution)/shard_map/ppermute | solution.py:17
  27.1 0.7 copy.48
  27.9 0.8 copy.47
  28.7 0.8 copy.36
  29.5 0.8 copy.37
  30.3 0.8 copy.38
  31.2 0.8 copy.39
  33.2 0.7 pad_maximum_fusion.9
  34.0 3.5 %collective-permute-start.4 = (bf16[2,8,20,128]{3,2,1,0:T(8,128)(2,1)S(1)}, bf16[2,8,20,128]{3,2,1,0:T(8,128)(2,1)S(1)}, u32[]{:S(2)}, u32[]{:S(2)}) collective-permute-start(bf16[2,8,20,128]{3,2,1,0:T(8,128)(2,1)S(1)} %pad_maximum_fusion.9), channel_id=1, source_target_pairs={{0,4},{4,8},{8,12},{1,5},{5,9},{9,13},{2,6},{6,10},{10,14},{3,7},{... | collective-permute-start | bytes 245768 | tf_op jit(solution)/shard_map/ppermute | solution.py:26
  37.5 0.8 pad_maximum_fusion.1
  38.8 0.9 collective-permute-done.4
  39.7 0.8 maximum_maximum_fusion
  41.9 0.2 convolution_add_fusion.21
  42.6 0.2 convolution_add_fusion.18
  43.3 0.2 convolution_add_fusion.15
  43.6 0.2 convolution_add_fusion.14
  43.8 0.2 convolution_add_fusion.13
  44.0 0.2 convolution_add_fusion.12
  44.3 0.3 fusion.9
  44.6 0.3 convolution_dynamic-update-slice_fusion.11
  44.9 4.5 %collective-permute-start.5 = (bf16[4,2,16,128]{3,2,1,0:T(8,128)(2,1)S(1)}, bf16[4,2,16,128]{3,2,1,0:T(8,128)(2,1)S(1)}, u32[]{:S(2)}, u32[]{:S(2)}) collective-permute-start(bf16[4,2,16,128]{3,2,1,0:T(8,128)(2,1)S(1)} %get-tuple-element.158), channel_id=1, source_target_pairs={{0,2},{1,3},{4,6},{5,7},{8,10},{9,11},{12,14},{13,15},{16,18},{17,... | collective-permute-start | bytes 98312 | tf_op jit(solution)/shard_map/ppermute | solution.py:17
  49.4 1.3 collective-permute-start.6
  50.7 0.3 convolution_dynamic-update-slice_fusion.10
  51.0 0.3 convolution_dynamic-update-slice_fusion.9
  51.3 0.3 convolution_dynamic-update-slice_fusion.8
  51.6 0.3 convolution_dynamic-update-slice_fusion.7
  51.9 0.3 convolution_dynamic-update-slice_fusion.6
  52.2 0.3 convolution_dynamic-update-slice_fusion.5
  52.5 0.3 convolution_dynamic-update-slice_fusion.4
  52.9 0.3 convolution_dynamic-update-slice_fusion.3
  53.2 0.3 convolution_dynamic-update-slice_fusion.2
  53.5 0.3 convolution_dynamic-update-slice_fusion.1
  53.8 0.3 convolution_dynamic-update-slice_fusion
  54.1 0.2 convolution_dynamic-update-slice_fusion.12
  54.3 0.9 collective-permute-done.6
  55.3 1.3 collective-permute-start.7
  56.6 1.4 collective-permute-start.8
  58.0 2.2 %multiply_bitcast_fusion = f32[1015808]{0:T(1024)} fusion(f32[7936,128]{1,0:T(8,128)S(1)} %convolution_dynamic-update-slice_fusion.12), kind=kLoop, calls=%fused_computation | loop fusion | flops 1015808 | bytes 8126464 | tf_op jit(solution)/shard_map/div | solution.py:156
  60.3 1.5 collective-permute-start.9
  62.4 5.4 %collective-permute-done.9 = bf16[2,8,20,128]{3,2,1,0:T(8,128)(2,1)S(1)} collective-permute-done((bf16[2,8,20,128]{3,2,1,0:T(8,128)(2,1)S(1)}, bf16[2,8,20,128]{3,2,1,0:T(8,128)(2,1)S(1)}, u32[]{:S(2)}, u32[]{:S(2)}) %collective-permute-start.9) | collective-permute-done | bytes 81952 | tf_op jit(solution)/shard_map/ppermute | solution.py:26
  70.0 0.2 convolution_add_fusion.7
  70.3 0.2 convolution_add_fusion.6
  70.5 0.2 convolution_add_fusion.5
  70.8 0.2 convolution_add_fusion.4
  71.0 0.2 convolution_add_fusion.3
  71.3 0.2 convolution_add_fusion.2
  71.5 0.2 convolution_add_fusion.1
  71.8 0.3 fusion.15
  72.1 1.0 convolution_multiply_fusion.1
  73.1 0.6 dynamic-slice
  74.4 34.5 %psum.15 = f32[128]{0:T(128)} all-reduce(f32[128]{0:T(128)S(1)} %broadcast_multiply_fusion), channel_id=1, replica_groups=mesh['groups'=2,'gx'=4,'gy'=2,'gz'=2] {'gx','gy','gz'}, use_global_device_ids=true, to_apply=%region_3.0 | all-reduce | flops 128 | bytes 1024 | tf_op jit(solution)/shard_map/psum | solution.py:168
  108.9 0.9 fusion.6
  109.8 75.5 %all-reduce.4.cloned.1.call-done = (f32[1015808]{0:T(1024)}, f32[128,128]{1,0:T(8,128)}) async-done(((f32[1015808]{0:T(1024)}, f32[128,128]{1,0:T(8,128)}), (f32[1015808]{0:T(1024)}, f32[128,128]{1,0:T(8,128)})) %all-reduce.4.cloned.1.call-update) | async-done | bytes 4128784
  185.3 1.7 dynamic-slice.1
  186.9 1.5 copy.159
  (103 shorter events, 6.9 us)
Async XLA Ops:
  7.2 0.9 copy-start
  7.2 178.1 %all-reduce.4.cloned.1.call-start = ((), (), s32[]{:S(2)}) async-start(), calls=%async_computation | async-start | bytes 8257536
  8.1 1.2 copy-start.15
  8.1 19.0 %copy-start.14 = (bf16[4,4,16,128]{3,2,1,0:T(8,128)(2,1)S(1)}, bf16[4,4,16,128]{3,2,1,0:T(8,128)(2,1)}, u32[]{:S(2)}) copy-start(bf16[4,4,16,128]{3,2,1,0:T(8,128)(2,1)} %param.7) | copy-start | bytes 196612
  9.3 12.2 %collective-permute-start = (bf16[4,2,16,128]{3,2,1,0:T(8,128)(2,1)S(1)}, bf16[4,2,16,128]{3,2,1,0:T(8,128)(2,1)S(1)}, u32[]{:S(2)}, u32[]{:S(2)}) collective-permute-start(bf16[4,2,16,128]{3,2,1,0:T(8,128)(2,1)S(1)} %get-tuple-element.160), channel_id=1, source_target_pairs={{0,2},{1,3},{4,6},{5,7},{8,10},{9,11},{12,14},{13,15},{16,18},{17,... | collective-permute-start | bytes 98312 | tf_op jit(solution)/shard_map/ppermute | solution.py:17
  14.2 7.3 %collective-permute-start.1 = (bf16[4,2,16,128]{3,2,1,0:T(8,128)(2,1)S(1)}, bf16[4,2,16,128]{3,2,1,0:T(8,128)(2,1)S(1)}, u32[]{:S(2)}, u32[]{:S(2)}) collective-permute-start(bf16[4,2,16,128]{3,2,1,0:T(8,128)(2,1)S(1)} %get-tuple-element.161), channel_id=1, source_target_pairs={{2,0},{3,1},{6,4},{7,5},{10,8},{11,9},{14,12},{15,13},{18,16},{19,... | collective-permute-start | bytes 98312 | tf_op jit(solution)/shard_map/ppermute | solution.py:18
  22.2 11.1 %collective-permute-start.3 = (bf16[4,8,2,128]{3,2,1,0:T(2,128)(2,1)}, bf16[4,8,2,128]{3,2,1,0:T(2,128)(2,1)S(1)}, u32[]{:S(2)}, u32[]{:S(2)}) collective-permute-start(bf16[4,8,2,128]{3,2,1,0:T(2,128)(2,1)} %get-tuple-element.152), channel_id=1, source_target_pairs={{1,0},{3,2},{5,4},{7,6},{9,8},{11,10},{13,12},{15,14},{17,16},{19,... | collective-permute-start | bytes 49160 | tf_op jit(solution)/shard_map/ppermute | solution.py:18
  23.5 9.8 %collective-permute-start.2 = (bf16[4,8,2,128]{3,2,1,0:T(2,128)(2,1)}, bf16[4,8,2,128]{3,2,1,0:T(2,128)(2,1)}, u32[]{:S(2)}, u32[]{:S(2)}) collective-permute-start(bf16[4,8,2,128]{3,2,1,0:T(2,128)(2,1)} %get-tuple-element.153), channel_id=1, source_target_pairs={{0,1},{2,3},{4,5},{6,7},{8,9},{10,11},{12,13},{14,15},{16,17},{18,... | collective-permute-start | bytes 49160 | tf_op jit(solution)/shard_map/ppermute | solution.py:17
  34.0 5.7 %collective-permute-start.4 = (bf16[2,8,20,128]{3,2,1,0:T(8,128)(2,1)S(1)}, bf16[2,8,20,128]{3,2,1,0:T(8,128)(2,1)S(1)}, u32[]{:S(2)}, u32[]{:S(2)}) collective-permute-start(bf16[2,8,20,128]{3,2,1,0:T(8,128)(2,1)S(1)} %pad_maximum_fusion.9), channel_id=1, source_target_pairs={{0,4},{4,8},{8,12},{1,5},{5,9},{9,13},{2,6},{6,10},{10,14},{3,7},{... | collective-permute-start | bytes 245768 | tf_op jit(solution)/shard_map/ppermute | solution.py:26
  38.4 3.2 %copy-start.7 = (bf16[5,128,128]{2,1,0:T(8,128)(2,1)S(1)}, bf16[5,128,128]{2,1,0:T(8,128)(2,1)}, u32[]{:S(2)}) copy-start(bf16[5,128,128]{2,1,0:T(8,128)(2,1)} %get-tuple-element.33) | copy-start | bytes 491524
  38.7 3.2 %copy-start.6 = (bf16[5,128,128]{2,1,0:T(8,128)(2,1)S(1)}, bf16[5,128,128]{2,1,0:T(8,128)(2,1)}, u32[]{:S(2)}) copy-start(bf16[5,128,128]{2,1,0:T(8,128)(2,1)} %get-tuple-element.32) | copy-start | bytes 491524
  40.5 1.6 copy-start.5
  40.6 1.8 copy-start.4
  40.6 2.0 %copy-start.2 = (bf16[5,128,128]{2,1,0:T(8,128)(2,1)S(1)}, bf16[5,128,128]{2,1,0:T(8,128)(2,1)}, u32[]{:S(2)}) copy-start(bf16[5,128,128]{2,1,0:T(8,128)(2,1)} %get-tuple-element.26) | copy-start | bytes 491524
  41.6 2.7 %copy-start.12 = (bf16[5,128,128]{2,1,0:T(8,128)(2,1)S(1)}, bf16[5,128,128]{2,1,0:T(8,128)(2,1)}, u32[]{:S(2)}) copy-start(bf16[5,128,128]{2,1,0:T(8,128)(2,1)} %get-tuple-element.29) | copy-start | bytes 491524
  41.6 2.7 %copy-start.16 = (f32[256]{0:T(256)S(1)}, f32[256]{0:T(256)}, u32[]{:S(2)}) copy-start(f32[256]{0:T(256)} %copy-done.15) | copy-start | bytes 3076
  44.9 9.4 %collective-permute-start.5 = (bf16[4,2,16,128]{3,2,1,0:T(8,128)(2,1)S(1)}, bf16[4,2,16,128]{3,2,1,0:T(8,128)(2,1)S(1)}, u32[]{:S(2)}, u32[]{:S(2)}) collective-permute-start(bf16[4,2,16,128]{3,2,1,0:T(8,128)(2,1)S(1)} %get-tuple-element.158), channel_id=1, source_target_pairs={{0,2},{1,3},{4,6},{5,7},{8,10},{9,11},{12,14},{13,15},{16,18},{17,... | collective-permute-start | bytes 98312 | tf_op jit(solution)/shard_map/ppermute | solution.py:17
  49.4 5.8 %collective-permute-start.6 = (bf16[4,2,16,128]{3,2,1,0:T(8,128)(2,1)S(1)}, bf16[4,2,16,128]{3,2,1,0:T(8,128)(2,1)S(1)}, u32[]{:S(2)}, u32[]{:S(2)}) collective-permute-start(bf16[4,2,16,128]{3,2,1,0:T(8,128)(2,1)S(1)} %get-tuple-element.159), channel_id=1, source_target_pairs={{2,0},{3,1},{6,4},{7,5},{10,8},{11,9},{14,12},{15,13},{18,16},{19,... | collective-permute-start | bytes 98312 | tf_op jit(solution)/shard_map/ppermute | solution.py:18
  55.3 4.9 %collective-permute-start.7 = (bf16[4,8,2,128]{3,2,1,0:T(2,128)(2,1)S(1)}, bf16[4,8,2,128]{3,2,1,0:T(2,128)(2,1)S(1)}, u32[]{:S(2)}, u32[]{:S(2)}) collective-permute-start(bf16[4,8,2,128]{3,2,1,0:T(2,128)(2,1)S(1)} %get-tuple-element.148), channel_id=1, source_target_pairs={{0,1},{2,3},{4,5},{6,7},{8,9},{10,11},{12,13},{14,15},{16,17},{18,... | collective-permute-start | bytes 49160 | tf_op jit(solution)/shard_map/ppermute | solution.py:17
  56.6 5.4 %copy-start.13 = (bf16[2,128,128]{2,1,0:T(8,128)(2,1)S(1)}, bf16[2,128,128]{2,1,0:T(8,128)(2,1)}, u32[]{:S(2)}) copy-start(bf16[2,128,128]{2,1,0:T(8,128)(2,1)} %copy.48) | copy-start | bytes 196612
  56.6 3.6 %collective-permute-start.8 = (bf16[4,8,2,128]{3,2,1,0:T(2,128)(2,1)S(1)}, bf16[4,8,2,128]{3,2,1,0:T(2,128)(2,1)S(1)}, u32[]{:S(2)}, u32[]{:S(2)}) collective-permute-start(bf16[4,8,2,128]{3,2,1,0:T(2,128)(2,1)S(1)} %get-tuple-element.149), channel_id=1, source_target_pairs={{1,0},{3,2},{5,4},{7,6},{9,8},{11,10},{13,12},{15,14},{17,16},{19,... | collective-permute-start | bytes 49160 | tf_op jit(solution)/shard_map/ppermute | solution.py:18
  60.3 7.5 %collective-permute-start.9 = (bf16[2,8,20,128]{3,2,1,0:T(8,128)(2,1)S(1)}, bf16[2,8,20,128]{3,2,1,0:T(8,128)(2,1)S(1)}, u32[]{:S(2)}, u32[]{:S(2)}) collective-permute-start(bf16[2,8,20,128]{3,2,1,0:T(8,128)(2,1)S(1)} %pad_maximum_fusion.5), channel_id=1, source_target_pairs={{4,0},{8,4},{12,8},{5,1},{9,5},{13,9},{6,2},{10,6},{14,10},{7,3},{... | collective-permute-start | bytes 245768 | tf_op jit(solution)/shard_map/ppermute | solution.py:26
  62.0 7.0 %copy-start.11 = (bf16[5,128,128]{2,1,0:T(8,128)(2,1)S(1)}, bf16[5,128,128]{2,1,0:T(8,128)(2,1)}, u32[]{:S(2)}) copy-start(bf16[5,128,128]{2,1,0:T(8,128)(2,1)} %copy.36) | copy-start | bytes 491524
  62.3 7.0 %copy-start.10 = (bf16[5,128,128]{2,1,0:T(8,128)(2,1)S(1)}, bf16[5,128,128]{2,1,0:T(8,128)(2,1)}, u32[]{:S(2)}) copy-start(bf16[5,128,128]{2,1,0:T(8,128)(2,1)} %copy.37) | copy-start | bytes 491524
  67.9 1.6 copy-start.9
  68.0 1.7 copy-start.8
  69.0 2.8 %copy-start.1 = (bf16[4,4,16,128]{3,2,1,0:T(8,128)(2,1)S(1)}, bf16[4,4,16,128]{3,2,1,0:T(8,128)(2,1)}, u32[]{:S(2)}) copy-start(bf16[4,4,16,128]{3,2,1,0:T(8,128)(2,1)} %param.6) | copy-start | bytes 196612
  69.0 2.8 %copy-start.3 = (bf16[5,128,128]{2,1,0:T(8,128)(2,1)S(1)}, bf16[5,128,128]{2,1,0:T(8,128)(2,1)}, u32[]{:S(2)}) copy-start(bf16[5,128,128]{2,1,0:T(8,128)(2,1)} %copy.47) | copy-start | bytes 491524
  71.0 2.1 %copy-start.17 = (u32[32]{0:T(128)S(1)}, u32[32]{0:T(128)}, u32[]{:S(2)}) copy-start(u32[32]{0:T(128)} %constant.15) | copy-start | bytes 388
Sparse Core Ops, SparseCore 0:
  73.2 111.9 all-reduce.3
where the time goes:
time: 196 us; the launch traced here: 195 us
  waiting for transfers between devices  82.8 us (42%)
  blocking collectives  34.5 us (18%)
  starting transfers between devices  24.6 us (13%)
  local copies, waits for them, and re-layouts  18.6 us (9%)
  between operations  15.6 us (8%)
  matrix products  12.9 us (7%)
  other arithmetic  6.33 us (3%)
    unnamed x2, waiting for transfers between devices  75.5 us
    psum x1, blocking collectives, local(): lax.psum((gamma_local, beta_local), ('gx', 'gy', 'gz'))  34.5 us
    ppermute x4, starting transfers between devices, padded_2(): before = lax.ppermute(last, axis, up)  14.3 us
    transpose x15, local copies, waits for them, and re-layouts, context_transposed(): jnp.transpose(kernel[first_tap:first_tap + count], (0, 2, 1))  9.94 us
    ppermute x2, waiting for transfers between devices, from_behind(): lax.ppermute(value, axis, [(source, source + steps) for source in range(l...  6.32 us
    unnamed x59, local copies, waits for them, and re-layouts  5.71 us
    ppermute x4, starting transfers between devices, padded_2(): after = lax.ppermute(leading, axis, down)  5.29 us
    ppermute x2, starting transfers between devices, from_behind(): lax.ppermute(value, axis, [(source, source + steps) for source in range(l...  4.96 us
  transfers between devices with their start and end apart: 11, of which 4 were waited for; matrix products, arithmetic and copies ran while one was open for 11% of the time, Pallas kernels for 0%

commit v1 on v0

--- a/solution.py
+++ b/solution.py
@@ -5,6 +5,11 @@
 from jax.sharding import PartitionSpec as P
 
 OB = 4
+
+
+def by_each_axis(array, one, other):
+    inner = lax.psum(array, one)
+    return lax.psum(inner, other)
 
 
 def padded_2(shard, sides, width):
@@ -165,7 +170,7 @@
         preferred_element_type=jnp.float32,
     )
     beta_local = -factor * jnp.sum(weighted, axis=0)
-    grad_gamma, grad_beta = lax.psum((gamma_local, beta_local), ("gx", "gy", "gz"))
+    grad_gamma, grad_beta = by_each_axis((gamma_local, beta_local), ("gy", "gz"), "gx")
     return (grad_features, grad_kernel, grad_gamma, grad_beta)
 
 

time: 196 us -> 263 us (1.34)
  waiting for transfers between devices: 82.8 us -> 163 us
  blocking collectives: 34.5 us -> 18.5 us
    psum x0 -> x2, waiting for transfers between devices: none -> 58.9 us  [the longest x1 34.2 us: by_each_axis(): return lax.psum(inner, other)]
    unnamed x2 -> x4, waiting for transfers between devices: 75.5 us -> 95.1 us
    psum x1 -> x2, blocking collectives: 34.5 us -> 18.5 us  [the longest x1 12.7 us: by_each_axis(): return lax.psum(inner, other)]
    unnamed x59 -> x61, local copies, waits for them, and re-layouts: 5.71 us -> 6.28 us
  transfers between devices with their start and end apart: 11 -> 13, of which waited for: 4 -> 7; matrix products, arithmetic and copies ran while one was open for 11% -> 9% of each run, Pallas kernels for 0% -> 0%
where the time goes in v1:
time: 263 us; the launch traced here: 262 us
  waiting for transfers between devices  163 us (62%)
  starting transfers between devices  24.6 us (9%)
  local copies, waits for them, and re-layouts  19 us (7%)
  blocking collectives  18.5 us (7%)
  between operations  15.3 us (6%)
  matrix products  13.1 us (5%)
  other arithmetic  8.55 us (3%)
    unnamed x4, waiting for transfers between devices  95.1 us
    psum x1, waiting for transfers between devices, by_each_axis(): return lax.psum(inner, other)  34.2 us
    psum x1, waiting for transfers between devices, by_each_axis(): inner = lax.psum(array, one)  24.7 us
    ppermute x4, starting transfers between devices, padded_2(): before = lax.ppermute(last, axis, up)  14.3 us
    psum x1, blocking collectives, by_each_axis(): return lax.psum(inner, other)  12.7 us
    transpose x15, local copies, waits for them, and re-layouts, context_transposed(): jnp.transpose(kernel[first_tap:first_tap + count], (0, 2, 1))  9.84 us
    unnamed x61, local copies, waits for them, and re-layouts  6.28 us
    ppermute x2, waiting for transfers between devices, from_behind(): lax.ppermute(value, axis, [(source, source + steps) for source in range(l...  6.21 us
  transfers between devices with their start and end apart: 13, of which 7 were waited for; matrix products, arithmetic and copies ran while one was open for 9% of the time, Pallas kernels for 0%

profile of v1, /device:TPU:0, one launch (start us, length us, event | category | flops | bytes accessed | tf_op | source)
XLA Modules:
  0.0 261.9 jit_solution(14108300536108189736)
XLA Ops:
  7.2 0.7 convert_bitcast_fusion
  8.1 1.2 fusion.12
  9.3 4.9 %collective-permute-start = (bf16[4,2,16,128]{3,2,1,0:T(8,128)(2,1)S(1)}, bf16[4,2,16,128]{3,2,1,0:T(8,128)(2,1)S(1)}, u32[]{:S(2)}, u32[]{:S(2)}) collective-permute-start(bf16[4,2,16,128]{3,2,1,0:T(8,128)(2,1)S(1)} %get-tuple-element.158), channel_id=1, source_target_pairs={{0,2},{1,3},{4,6},{5,7},{8,10},{9,11},{12,14},{13,15},{16,18},{17,... | collective-permute-start | bytes 98312 | tf_op jit(solution)/shard_map/ppermute | solution.py:22
  14.2 1.3 collective-permute-start.1
  15.5 2.2 fusion.16
  17.7 2.9 %slice_bitcast_fusion.1 = (bf16[5,128,128]{1,2,0:T(8,128)(2,1)S(1)}, bf16[5,128,128]{1,2,0:T(8,128)(2,1)S(1)}, bf16[5,128,128]{1,2,0:T(8,128)(2,1)S(1)}, bf16[5,...) fusion(bf16[62,128,128]{2,1,0:T(8,128)(2,1)} %param.9), kind=kLoop, calls=%fused_computation.212 | loop fusion | bytes 5079040 | tf_op jit(solution)/shard_map/transpose | solution.py:99
  20.6 0.9 slice_bitcast_fusion
  21.5 0.6 pad_maximum_fusion.18
  22.1 1.3 collective-permute-start.3
  23.4 3.6 %collective-permute-start.2 = (bf16[4,8,2,128]{3,2,1,0:T(2,128)(2,1)}, bf16[4,8,2,128]{3,2,1,0:T(2,128)(2,1)}, u32[]{:S(2)}, u32[]{:S(2)}) collective-permute-start(bf16[4,8,2,128]{3,2,1,0:T(2,128)(2,1)} %get-tuple-element.151), channel_id=1, source_target_pairs={{0,1},{2,3},{4,5},{6,7},{8,9},{10,11},{12,13},{14,15},{16,17},{18,... | collective-permute-start | bytes 49160 | tf_op jit(solution)/shard_map/ppermute | solution.py:22
  27.0 0.7 copy.48
  27.8 0.8 copy.47
  28.6 0.8 copy.36
  29.4 0.8 copy.37
  30.3 0.8 copy.38
  31.1 0.8 copy.39
  33.1 0.7 pad_maximum_fusion.9
  33.9 3.5 %collective-permute-start.4 = (bf16[2,8,20,128]{3,2,1,0:T(8,128)(2,1)S(1)}, bf16[2,8,20,128]{3,2,1,0:T(8,128)(2,1)S(1)}, u32[]{:S(2)}, u32[]{:S(2)}) collective-permute-start(bf16[2,8,20,128]{3,2,1,0:T(8,128)(2,1)S(1)} %pad_maximum_fusion.9), channel_id=1, source_target_pairs={{0,4},{4,8},{8,12},{1,5},{5,9},{9,13},{2,6},{6,10},{10,14},{3,7},{... | collective-permute-start | bytes 245768 | tf_op jit(solution)/shard_map/ppermute | solution.py:31
  37.4 0.8 pad_maximum_fusion.1
  38.7 0.9 collective-permute-done.4
  39.6 0.8 maximum_maximum_fusion
  42.6 0.2 convolution_add_fusion.18
  42.8 0.2 convolution_add_fusion.17
  43.1 0.2 convolution_add_fusion.16
  43.3 0.2 convolution_add_fusion.15
  43.6 0.2 convolution_add_fusion.14
  43.8 0.2 convolution_add_fusion.13
  44.1 0.2 convolution_add_fusion.12
  44.4 0.2 fusion.9
  44.6 0.3 convolution_dynamic-update-slice_fusion.11
  44.9 4.5 %collective-permute-start.5 = (bf16[4,2,16,128]{3,2,1,0:T(8,128)(2,1)S(1)}, bf16[4,2,16,128]{3,2,1,0:T(8,128)(2,1)S(1)}, u32[]{:S(2)}, u32[]{:S(2)}) collective-permute-start(bf16[4,2,16,128]{3,2,1,0:T(8,128)(2,1)S(1)} %get-tuple-element.156), channel_id=1, source_target_pairs={{0,2},{1,3},{4,6},{5,7},{8,10},{9,11},{12,14},{13,15},{16,18},{17,... | collective-permute-start | bytes 98312 | tf_op jit(solution)/shard_map/ppermute | solution.py:22
  49.5 1.3 collective-permute-start.6
  50.8 0.3 convolution_dynamic-update-slice_fusion.10
  51.1 0.3 convolution_dynamic-update-slice_fusion.9
  51.4 0.3 convolution_dynamic-update-slice_fusion.8
  51.7 0.3 convolution_dynamic-update-slice_fusion.7
  52.0 0.3 convolution_dynamic-update-slice_fusion.6
  52.3 0.3 convolution_dynamic-update-slice_fusion.5
  52.6 0.3 convolution_dynamic-update-slice_fusion.4
  52.9 0.3 convolution_dynamic-update-slice_fusion.3
  53.2 0.3 convolution_dynamic-update-slice_fusion.2
  53.5 0.3 convolution_dynamic-update-slice_fusion.1
  53.8 0.3 convolution_dynamic-update-slice_fusion
  54.1 1.2 collective-permute-done.6
  55.3 1.3 collective-permute-start.7
  56.6 1.3 collective-permute-start.8
  58.2 1.5 collective-permute-done.8
  59.8 1.5 collective-permute-start.9
  61.9 5.3 %collective-permute-done.9 = bf16[2,8,20,128]{3,2,1,0:T(8,128)(2,1)S(1)} collective-permute-done((bf16[2,8,20,128]{3,2,1,0:T(8,128)(2,1)S(1)}, bf16[2,8,20,128]{3,2,1,0:T(8,128)(2,1)S(1)}, u32[]{:S(2)}, u32[]{:S(2)}) %collective-permute-start.9) | collective-permute-done | bytes 81952 | tf_op jit(solution)/shard_map/ppermute | solution.py:31
  69.2 0.2 convolution_add_fusion.8
  71.0 0.2 convolution_add_fusion.1
  71.3 0.3 fusion.15
  71.5 1.0 convolution_multiply_fusion.1
  72.6 4.4 %multiply_bitcast_fusion = f32[1015808]{0:T(1024)} fusion(f32[7936,128]{1,0:T(8,128)} %copy-done.1), kind=kLoop, calls=%fused_computation | loop fusion | flops 1015808 | bytes 8126464 | tf_op jit(solution)/shard_map/div | solution.py:161
  77.1 0.6 copy-done.18
  77.7 0.6 dynamic-slice
  78.9 0.9 fusion.6
  79.8 24.7 %all-reduce.5.cloned.1.call-done = f32[128,128]{1,0:T(8,128)} async-done(((f32[128,128]{1,0:T(8,128)}), f32[128,128]{1,0:T(8,128)}) %all-reduce.5.cloned.1.call-update) | async-done | bytes 65552 | tf_op jit(solution)/shard_map/psum | solution.py:11
  104.6 5.8 %psum.30 = f32[128]{0:T(128)S(1)} all-reduce(f32[128]{0:T(128)S(1)} %broadcast_multiply_fusion), channel_id=1, replica_groups=mesh['groups'=2,'gx'=4,'gy'=2,'gz'=2] {'gy','gz'}, use_global_device_ids=true, to_apply=%region_4.0 | all-reduce | flops 128 | bytes 1024 | tf_op jit(solution)/shard_map/psum | solution.py:11
  110.4 12.7 %psum.31 = f32[128]{0:T(128)} all-reduce(f32[128]{0:T(128)S(1)} %psum.30), channel_id=1, replica_groups=mesh['groups'=2,'gx'=4,'gy'=2,'gz'=2] {'gx'}, use_global_device_ids=true, to_apply=%region_5.0 | all-reduce | flops 128 | bytes 1024 | tf_op jit(solution)/shard_map/psum | solution.py:12
  123.1 95.0 %all-reduce.9.cloned.1.call-done = f32[1015808]{0:T(1024)} async-done(((f32[1015808]{0:T(1024)}), f32[1015808]{0:T(1024)}) %all-reduce.9.cloned.1.call-update) | async-done | bytes 4063248
  218.1 1.7 dynamic-slice.1
  219.8 34.2 %all-reduce.7.cloned.1.call-done = f32[128,128]{1,0:T(8,128)} async-done(((f32[128,128]{1,0:T(8,128)}), f32[128,128]{1,0:T(8,128)}) %all-reduce.7.cloned.1.call-update) | async-done | bytes 65552 | tf_op jit(solution)/shard_map/psum | solution.py:12
  253.9 1.5 copy.160
  (112 shorter events, 8.3 us)
Async XLA Ops:
  7.2 0.9 copy-start
  7.2 97.4 %all-reduce.5.cloned.1.call-start = ((), (), s32[]{:S(2)}) async-start(), calls=%async_computation | async-start | bytes 131072 | tf_op jit(solution)/shard_map/psum | solution.py:11
  8.1 1.2 copy-start.16
  8.1 18.9 %copy-start.15 = (bf16[4,4,16,128]{3,2,1,0:T(8,128)(2,1)S(1)}, bf16[4,4,16,128]{3,2,1,0:T(8,128)(2,1)}, u32[]{:S(2)}) copy-start(bf16[4,4,16,128]{3,2,1,0:T(8,128)(2,1)} %param.7) | copy-start | bytes 196612
  9.3 12.1 %collective-permute-start = (bf16[4,2,16,128]{3,2,1,0:T(8,128)(2,1)S(1)}, bf16[4,2,16,128]{3,2,1,0:T(8,128)(2,1)S(1)}, u32[]{:S(2)}, u32[]{:S(2)}) collective-permute-start(bf16[4,2,16,128]{3,2,1,0:T(8,128)(2,1)S(1)} %get-tuple-element.158), channel_id=1, source_target_pairs={{0,2},{1,3},{4,6},{5,7},{8,10},{9,11},{12,14},{13,15},{16,18},{17,... | collective-permute-start | bytes 98312 | tf_op jit(solution)/shard_map/ppermute | solution.py:22
  14.2 7.2 %collective-permute-start.1 = (bf16[4,2,16,128]{3,2,1,0:T(8,128)(2,1)S(1)}, bf16[4,2,16,128]{3,2,1,0:T(8,128)(2,1)S(1)}, u32[]{:S(2)}, u32[]{:S(2)}) collective-permute-start(bf16[4,2,16,128]{3,2,1,0:T(8,128)(2,1)S(1)} %get-tuple-element.159), channel_id=1, source_target_pairs={{2,0},{3,1},{6,4},{7,5},{10,8},{11,9},{14,12},{15,13},{18,16},{19,... | collective-permute-start | bytes 98312 | tf_op jit(solution)/shard_map/ppermute | solution.py:23
  22.1 11.0 %collective-permute-start.3 = (bf16[4,8,2,128]{3,2,1,0:T(2,128)(2,1)}, bf16[4,8,2,128]{3,2,1,0:T(2,128)(2,1)S(1)}, u32[]{:S(2)}, u32[]{:S(2)}) collective-permute-start(bf16[4,8,2,128]{3,2,1,0:T(2,128)(2,1)} %get-tuple-element.150), channel_id=1, source_target_pairs={{1,0},{3,2},{5,4},{7,6},{9,8},{11,10},{13,12},{15,14},{17,16},{19,... | collective-permute-start | bytes 49160 | tf_op jit(solution)/shard_map/ppermute | solution.py:23
  23.4 9.7 %collective-permute-start.2 = (bf16[4,8,2,128]{3,2,1,0:T(2,128)(2,1)}, bf16[4,8,2,128]{3,2,1,0:T(2,128)(2,1)}, u32[]{:S(2)}, u32[]{:S(2)}) collective-permute-start(bf16[4,8,2,128]{3,2,1,0:T(2,128)(2,1)} %get-tuple-element.151), channel_id=1, source_target_pairs={{0,1},{2,3},{4,5},{6,7},{8,9},{10,11},{12,13},{14,15},{16,17},{18,... | collective-permute-start | bytes 49160 | tf_op jit(solution)/shard_map/ppermute | solution.py:22
  33.9 5.7 %collective-permute-start.4 = (bf16[2,8,20,128]{3,2,1,0:T(8,128)(2,1)S(1)}, bf16[2,8,20,128]{3,2,1,0:T(8,128)(2,1)S(1)}, u32[]{:S(2)}, u32[]{:S(2)}) collective-permute-start(bf16[2,8,20,128]{3,2,1,0:T(8,128)(2,1)S(1)} %pad_maximum_fusion.9), channel_id=1, source_target_pairs={{0,4},{4,8},{8,12},{1,5},{5,9},{9,13},{2,6},{6,10},{10,14},{3,7},{... | collective-permute-start | bytes 245768 | tf_op jit(solution)/shard_map/ppermute | solution.py:31
  38.3 3.2 %copy-start.8 = (bf16[5,128,128]{2,1,0:T(8,128)(2,1)S(1)}, bf16[5,128,128]{2,1,0:T(8,128)(2,1)}, u32[]{:S(2)}) copy-start(bf16[5,128,128]{2,1,0:T(8,128)(2,1)} %get-tuple-element.31) | copy-start | bytes 491524
  38.6 3.2 %copy-start.7 = (bf16[5,128,128]{2,1,0:T(8,128)(2,1)S(1)}, bf16[5,128,128]{2,1,0:T(8,128)(2,1)}, u32[]{:S(2)}) copy-start(bf16[5,128,128]{2,1,0:T(8,128)(2,1)} %get-tuple-element.30) | copy-start | bytes 491524
  40.4 1.6 copy-start.6
  40.5 1.8 copy-start.5
  40.5 2.1 copy-start.3
  41.5 2.8 %copy-start.13 = (bf16[5,128,128]{2,1,0:T(8,128)(2,1)S(1)}, bf16[5,128,128]{2,1,0:T(8,128)(2,1)}, u32[]{:S(2)}) copy-start(bf16[5,128,128]{2,1,0:T(8,128)(2,1)} %get-tuple-element.27) | copy-start | bytes 491524
  41.5 2.8 %copy-start.17 = (f32[256]{0:T(256)S(1)}, f32[256]{0:T(256)}, u32[]{:S(2)}) copy-start(f32[256]{0:T(256)} %copy-done.16) | copy-start | bytes 3076
  44.9 9.2 %collective-permute-start.5 = (bf16[4,2,16,128]{3,2,1,0:T(8,128)(2,1)S(1)}, bf16[4,2,16,128]{3,2,1,0:T(8,128)(2,1)S(1)}, u32[]{:S(2)}, u32[]{:S(2)}) collective-permute-start(bf16[4,2,16,128]{3,2,1,0:T(8,128)(2,1)S(1)} %get-tuple-element.156), channel_id=1, source_target_pairs={{0,2},{1,3},{4,6},{5,7},{8,10},{9,11},{12,14},{13,15},{16,18},{17,... | collective-permute-start | bytes 98312 | tf_op jit(solution)/shard_map/ppermute | solution.py:22
  49.5 5.8 %collective-permute-start.6 = (bf16[4,2,16,128]{3,2,1,0:T(8,128)(2,1)S(1)}, bf16[4,2,16,128]{3,2,1,0:T(8,128)(2,1)S(1)}, u32[]{:S(2)}, u32[]{:S(2)}) collective-permute-start(bf16[4,2,16,128]{3,2,1,0:T(8,128)(2,1)S(1)} %get-tuple-element.157), channel_id=1, source_target_pairs={{2,0},{3,1},{6,4},{7,5},{10,8},{11,9},{14,12},{15,13},{18,16},{19,... | collective-permute-start | bytes 98312 | tf_op jit(solution)/shard_map/ppermute | solution.py:23
  51.7 9.8 %copy-start.14 = (bf16[2,128,128]{2,1,0:T(8,128)(2,1)S(1)}, bf16[2,128,128]{2,1,0:T(8,128)(2,1)}, u32[]{:S(2)}) copy-start(bf16[2,128,128]{2,1,0:T(8,128)(2,1)} %copy.48) | copy-start | bytes 196612
  55.3 2.8 %collective-permute-start.7 = (bf16[4,8,2,128]{3,2,1,0:T(2,128)(2,1)S(1)}, bf16[4,8,2,128]{3,2,1,0:T(2,128)(2,1)S(1)}, u32[]{:S(2)}, u32[]{:S(2)}) collective-permute-start(bf16[4,8,2,128]{3,2,1,0:T(2,128)(2,1)S(1)} %get-tuple-element.146), channel_id=1, source_target_pairs={{0,1},{2,3},{4,5},{6,7},{8,9},{10,11},{12,13},{14,15},{16,17},{18,... | collective-permute-start | bytes 49160 | tf_op jit(solution)/shard_map/ppermute | solution.py:22
  56.6 3.1 %collective-permute-start.8 = (bf16[4,8,2,128]{3,2,1,0:T(2,128)(2,1)S(1)}, bf16[4,8,2,128]{3,2,1,0:T(2,128)(2,1)S(1)}, u32[]{:S(2)}, u32[]{:S(2)}) collective-permute-start(bf16[4,8,2,128]{3,2,1,0:T(2,128)(2,1)S(1)} %get-tuple-element.147), channel_id=1, source_target_pairs={{1,0},{3,2},{5,4},{7,6},{9,8},{11,10},{13,12},{15,14},{17,16},{19,... | collective-permute-start | bytes 49160 | tf_op jit(solution)/shard_map/ppermute | solution.py:23
  58.2 3.7 %copy-start.1 = (f32[7936,128]{1,0:T(8,128)}, f32[7936,128]{1,0:T(8,128)S(1)}, u32[]{:S(2)}) copy-start(f32[7936,128]{1,0:T(8,128)S(1)} %convolution_dynamic-update-slice_fusion.12) | copy-start | bytes 12189700
  59.8 7.4 %collective-permute-start.9 = (bf16[2,8,20,128]{3,2,1,0:T(8,128)(2,1)S(1)}, bf16[2,8,20,128]{3,2,1,0:T(8,128)(2,1)S(1)}, u32[]{:S(2)}, u32[]{:S(2)}) collective-permute-start(bf16[2,8,20,128]{3,2,1,0:T(8,128)(2,1)S(1)} %pad_maximum_fusion.5), channel_id=1, source_target_pairs={{4,0},{8,4},{12,8},{5,1},{9,5},{13,9},{6,2},{10,6},{14,10},{7,3},{... | collective-permute-start | bytes 245768 | tf_op jit(solution)/shard_map/ppermute | solution.py:31
  61.5 6.9 %copy-start.12 = (bf16[5,128,128]{2,1,0:T(8,128)(2,1)S(1)}, bf16[5,128,128]{2,1,0:T(8,128)(2,1)}, u32[]{:S(2)}) copy-start(bf16[5,128,128]{2,1,0:T(8,128)(2,1)} %copy.36) | copy-start | bytes 491524
  61.8 6.9 %copy-start.11 = (bf16[5,128,128]{2,1,0:T(8,128)(2,1)S(1)}, bf16[5,128,128]{2,1,0:T(8,128)(2,1)}, u32[]{:S(2)}) copy-start(bf16[5,128,128]{2,1,0:T(8,128)(2,1)} %copy.37) | copy-start | bytes 491524
  67.3 1.6 copy-start.10
  67.4 1.8 copy-start.9
  68.4 2.8 %copy-start.2 = (bf16[4,4,16,128]{3,2,1,0:T(8,128)(2,1)S(1)}, bf16[4,4,16,128]{3,2,1,0:T(8,128)(2,1)}, u32[]{:S(2)}) copy-start(bf16[4,4,16,128]{3,2,1,0:T(8,128)(2,1)} %param.6) | copy-start | bytes 196612
  68.4 2.8 %copy-start.4 = (bf16[5,128,128]{2,1,0:T(8,128)(2,1)S(1)}, bf16[5,128,128]{2,1,0:T(8,128)(2,1)}, u32[]{:S(2)}) copy-start(bf16[5,128,128]{2,1,0:T(8,128)(2,1)} %copy.47) | copy-start | bytes 491524
  72.6 145.6 %all-reduce.9.cloned.1.call-start = ((), (), s32[]{:S(2)}) async-start(), calls=%async_computation.2 | async-start | bytes 8126464
  77.0 0.7 copy-start.18
  77.1 176.9 %all-reduce.7.cloned.1.call-start = ((), (), s32[]{:S(2)}) async-start(), calls=%async_computation.1 | async-start | bytes 131072 | tf_op jit(solution)/shard_map/psum | solution.py:12
Sparse Core Ops, SparseCore 0:
  72.7 31.8 all-reduce.4
  108.2 109.8 all-reduce.8
  220.5 33.4 all-reduce.6
